TPU v7x, 256 devices: a whole 4x4x8 slice. The times are simulated.
256 devices in a mesh: seq: 32 (over z_hi, x, core), tensor: 8 (over y, z_lo).
Axes of the slice: x: 4, y: 4, z: 8 (z_hi: 4, z_lo: 2; z = z_hi * 2 + z_lo), core: 2. Of those that a mesh axis runs over, the one named last changes fastest.
Arguments:
- tokens: bfloat16 [4096, 2048], P('seq'), may hold values from -6 to 6
- lengths: int32 [8], replicated, may hold values from 1 to 2048, 4096 in all
- page_table: int32 [256], replicated, may hold values from 0 to 255, each once
- attention_gain: float32 [2048], replicated, may hold values from 0.25 to 1.75
- query_weight: bfloat16 [2048, 2048], P(None, 'tensor')
- key_weight: bfloat16 [2048, 2048], P(None, 'tensor')
- value_weight: bfloat16 [2048, 2048], P(None, 'tensor'), may hold values from -0.125 to 0.125
- out_weight: bfloat16 [2048, 2048], P('tensor'), may hold values from -0.125 to 0.125
- expert_gain: float32 [2048], replicated, may hold values from 0.25 to 1.75
- router_weight: bfloat16 [2048, 64], replicated, may hold values from -0.03125 to 0.03125
- expert_ids: int32 [4096, 8], P('seq'), may hold values from 0 to 63, all different within a row; in each aligned block of 128 rows (0 to 127, 128 to 255, ...) at most 24 rows name the same one
- gate_weight: bfloat16 [64, 2048, 1024], P('seq', None, 'tensor'), may hold values from -0.125 to 0.125
- up_weight: bfloat16 [64, 2048, 1024], P('seq', None, 'tensor'), may hold values from -0.125 to 0.125
- down_weight: bfloat16 [64, 1024, 2048], P('seq', 'tensor'), may hold values from -6 to 6
Outputs:
- layer_out: bfloat16 [4096, 2048], P('seq')
- key_cache: bfloat16 [256, 16, 2048], P('seq', None, 'tensor')
- value_cache: bfloat16 [256, 16, 2048], P('seq', None, 'tensor')
Inputs may be any that keep to these rules, and one draw needn't show every extreme that they name: The 8 lengths sum to 4096; the longest is exactly 2048. `page_table`: every page number appears once. `expert_ids`: each token names 8 different experts; among the 128 tokens of one index of seq no expert is named more than 24 times, a bound that some block reaches.
All inputs are finite; a program needn't handle non-finite values.
Results may differ from a plain program's by a relative error of at most 0.023.
Values may be sent and summed in bfloat16 or wider, within the bound.
A program may use at most 128 MiB of HBM per device.

v0:
```python
import jax
import jax.numpy as jnp
from jax import lax
from jax.sharding import PartitionSpec as P

HEAD_DIM = 128
PAGE = 16
epsilon = 1e-05
rope_base = 10000.0


def rms_scale(matrix, scaling):
    mean_square = jnp.mean(matrix * matrix, axis=-1, keepdims=True)
    return matrix * lax.rsqrt(mean_square + epsilon) * scaling


def segment_info(lengths, places):
    starts = jnp.cumsum(lengths) - lengths
    inside = (places[:, None] >= starts[None, :]).astype(jnp.int32)
    segment = jnp.sum(inside, axis=1) - 1
    slot_ids = jnp.arange(starts.shape[0], dtype=jnp.int32)
    seg_start = jnp.sum(
        jnp.where(slot_ids[None, :] == segment[:, None], starts[None, :], 0), axis=1
    )
    return (segment, places - seg_start)


def rotate(matrix, position):
    half_dim = matrix.shape[-1] // 2
    frequency = jnp.exp(
        -jnp.log(rope_base) * jnp.arange(half_dim, dtype=jnp.float32) * (2.0 / matrix.shape[-1])
    )
    angles = position.astype(jnp.float32)[:, None] * frequency[None, :]
    cosine = jnp.cos(angles)[:, None, :]
    sine_part = jnp.sin(angles)[:, None, :]
    first_half = matrix[..., :half_dim]
    second = matrix[..., half_dim:]
    return jnp.concatenate(
        [first_half * cosine - second * sine_part, second * cosine + first_half * sine_part],
        axis=-1,
    )


def local(
    tokens,
    lengths,
    page_table,
    attention_gain,
    query_weight,
    key_weight,
    value_weight,
    out_weight,
    expert_gain,
    router_weight,
    expert_ids,
    gate_weight,
    up_weight,
    down_weight,
):
    row_count = tokens.shape[0]
    feature_count = tokens.shape[1]
    span_size = query_weight.shape[1]
    head_count = span_size // HEAD_DIM
    shard_id = lax.axis_index("seq")
    places = shard_id * row_count + jnp.arange(row_count, dtype=jnp.int32)
    segment, position = segment_info(lengths, places)
    stream = tokens.astype(jnp.float32)
    normed = rms_scale(stream, attention_gain).astype(jnp.bfloat16)
    queries = rotate(
        jnp.dot(normed, query_weight, preferred_element_type=jnp.float32).reshape(
            row_count, head_count, HEAD_DIM
        ),
        position,
    ).astype(jnp.bfloat16)
    key_rows = (
        rotate(
            jnp.dot(normed, key_weight, preferred_element_type=jnp.float32).reshape(
                row_count, head_count, HEAD_DIM
            ),
            position,
        )
        .astype(jnp.bfloat16)
        .reshape(row_count, span_size)
    )
    value_rows = jnp.dot(normed, value_weight, preferred_element_type=jnp.float32).astype(
        jnp.bfloat16
    )
    page_rows = row_count // PAGE
    my_pages = shard_id * page_rows + jnp.arange(page_rows, dtype=jnp.int32)
    owned = (page_table[None, :] == my_pages[:, None]).astype(jnp.bfloat16)
    score_scale = HEAD_DIM ** (-0.5)
    state = (
        jnp.full((head_count, row_count), -1e30, jnp.float32),
        jnp.zeros((head_count, row_count), jnp.float32),
        jnp.zeros((head_count, row_count, HEAD_DIM), jnp.float32),
    )
    key_piece = lax.all_gather(key_rows, "seq", axis=0, tiled=True)
    value_piece = lax.all_gather(value_rows, "seq", axis=0, tiled=True)
    piece_rows = key_piece.shape[0]
    key_pages = jnp.dot(
        owned,
        key_piece.reshape(piece_rows // PAGE, PAGE * span_size),
        preferred_element_type=jnp.float32,
    )
    value_pages = jnp.dot(
        owned,
        value_piece.reshape(piece_rows // PAGE, PAGE * span_size),
        preferred_element_type=jnp.float32,
    )
    row_peak, row_total, weighted = state
    piece_rows = key_piece.shape[0]
    key_places = jnp.arange(piece_rows, dtype=jnp.int32)
    key_segments, _ = segment_info(lengths, key_places)
    scores = (
        jnp.einsum(
            "qhd,khd->hqk",
            queries,
            key_piece.reshape(piece_rows, head_count, HEAD_DIM),
            preferred_element_type=jnp.float32,
        )
        * score_scale
    )
    allowed = (
        (segment[:, None] == key_segments[None, :]) & (key_places[None, :] <= places[:, None])
    )[None]
    new_peak = jnp.maximum(row_peak, jnp.max(jnp.where(allowed, scores, -1e30), axis=-1))
    raised = jnp.where(allowed, jnp.exp(scores - new_peak[:, :, None]), 0.0)
    row_total = jnp.sum(raised, axis=-1)
    weighted = jnp.einsum(
        "hqk,khd->hqd",
        raised.astype(jnp.bfloat16),
        value_piece.reshape(piece_rows, head_count, HEAD_DIM),
        preferred_element_type=jnp.float32,
    )
    state = (new_peak, row_total, weighted)
    state, key_pages, value_pages = (state, key_pages, value_pages)
    _, row_total, weighted = state
    attended = (
        jnp.transpose(weighted / row_total[:, :, None], (1, 0, 2))
        .reshape(row_count, span_size)
        .astype(jnp.bfloat16)
    )
    head_part = jnp.dot(attended, out_weight, preferred_element_type=jnp.float32)
    hidden = stream + lax.psum(head_part.astype(jnp.bfloat16), "tensor").astype(jnp.float32)
    moe_input = rms_scale(hidden, expert_gain).astype(jnp.bfloat16)
    expert_count = router_weight.shape[1]
    probability = jax.nn.softmax(
        jnp.dot(moe_input, router_weight, preferred_element_type=jnp.float32), axis=-1
    )
    expert_range = jnp.arange(expert_count, dtype=jnp.int32)
    chosen = jnp.sum(
        jnp.where(
            expert_ids[:, :, None] == expert_range[None, None, :], probability[:, None, :], 0.0
        ),
        axis=-1,
    )
    top_count = expert_ids.shape[1]
    flat_ids = expert_ids.reshape(-1)
    onehot = (flat_ids[:, None] == expert_range[None, :]).astype(jnp.int32)
    slot_rank = jnp.sum(jnp.cumsum(onehot, axis=0) * onehot, axis=1) - 1
    members = lax.axis_size("tensor")
    sources = lax.axis_size("seq")
    local_count = gate_weight.shape[0]
    base_room = row_count * top_count * 3 // (2 * expert_count)
    capacity = members * ((base_room + members - 1) // members)
    owners = jnp.arange(row_count * top_count, dtype=jnp.int32) // top_count
    slot_index = flat_ids * capacity + slot_rank
    row_table = (
        jnp.full((expert_count * capacity,), row_count, jnp.int32).at[slot_index].set(owners)
    )
    padded = jnp.concatenate([moe_input, jnp.zeros((1, feature_count), jnp.bfloat16)], axis=0)
    outgoing = padded[row_table].reshape(sources, local_count, capacity, feature_count)
    arrived = lax.all_to_all(outgoing, "seq", split_axis=0, concat_axis=0, tiled=True)
    gate_out = jnp.einsum(
        "sjnd,jdf->sjnf", arrived, gate_weight, preferred_element_type=jnp.float32
    )
    up_out = jnp.einsum("sjnd,jdf->sjnf", arrived, up_weight, preferred_element_type=jnp.float32)
    activation = (jax.nn.silu(gate_out) * up_out).astype(jnp.bfloat16)
    returned = lax.all_to_all(
        jnp.einsum(
            "sjnf,jfd->sjnd", activation, down_weight, preferred_element_type=jnp.float32
        ).astype(jnp.bfloat16),
        "seq",
        split_axis=0,
        concat_axis=0,
        tiled=True,
    )
    flat_rows = returned.reshape(expert_count * capacity, feature_count)
    picked = flat_rows[slot_index].astype(jnp.float32)
    mixture_part = jnp.sum(
        picked.reshape(row_count, top_count, feature_count) * chosen[:, :, None], axis=1
    )
    mixture = lax.psum(mixture_part.astype(jnp.bfloat16), "tensor").astype(jnp.float32)
    layer_out = (hidden + mixture).astype(jnp.bfloat16)
    key_cache = key_pages.reshape(page_rows, PAGE, span_size).astype(jnp.bfloat16)
    value_cache = value_pages.reshape(page_rows, PAGE, span_size).astype(jnp.bfloat16)
    return (layer_out, key_cache, value_cache)


def solution(mesh):
    return jax.shard_map(
        local,
        mesh=mesh,
        in_specs=(
            P("seq", None),
            P(),
            P(),
            P(),
            P(None, "tensor"),
            P(None, "tensor"),
            P(None, "tensor"),
            P("tensor", None),
            P(),
            P(),
            P("seq", None),
            P("seq", None, "tensor"),
            P("seq", None, "tensor"),
            P("seq", "tensor", None),
        ),
        out_specs=(P("seq", None), P("seq", None, "tensor"), P("seq", None, "tensor")),
        check_vma=False,
    )
```

profile of v0, /device:TPU:2, one launch (start us, length us, event | category | flops | bytes accessed | tf_op | source)
XLA Modules:
  0.0 651.1 jit_solution(417091453030510193)
XLA Ops:
  7.3 0.9 reduce-window.19
  8.2 0.7 bitcast_subtract_fusion
  8.9 0.1 convert_reduce_fusion.1
  9.0 0.1 select_reduce_fusion.2
  9.1 1.2 fusion.34
  10.3 1.8 fusion.75
  12.1 0.1 reshape.271
  12.2 1.8 fusion.77
  13.9 0.1 reshape.270
  14.0 0.3 multiply_cosine_fusion
  14.3 0.3 fusion.79
  14.6 0.1 subtract_convert_fusion.1
  14.7 0.1 pad_maximum_fusion
  14.8 0.7 copy.74
  15.7 2.2 convolution_convert_fusion.3
  18.0 0.1 copy.78
  18.1 0.1 eq.91
  18.2 0.1 eq.87
  18.3 0.1 copy.77
  18.4 0.1 mul.205
  18.5 18.0 %reduce-window.20 = s32[64,8,128]{2,1,0:T(8,128)S(1)} reduce-window(s32[64,8,128]{2,1,0:T(8,128)S(1)} %fusion.52, s32[]{:T(128)} %constant.30.clone.1), window={size=1x1x128 pad=0_0x0_0x127_0}, to_apply=%region_9.10 | reduce-window | flops 8323072 | bytes 524292 | tf_op jit(solution)/shard_map/reduce-window.1
  36.5 0.1 slice.32
  36.6 0.1 copy.80
  36.8 0.1 copy.81
  36.9 0.1 convert_reduce_fusion
  37.0 0.1 broadcast_add_fusion
  37.3 0.5 fusion.11
  37.8 35.6 %all-gather.3.cloned.1.call-done = bf16[4096,256]{0,1:T(8,128)(2,1)} async-done(((bf16[128,256]{0,1:T(8,128)(2,1)}), bf16[4096,256]{0,1:T(8,128)(2,1)}) %all-gather.3.cloned.1.call-update) | async-done | bytes 2097168 | tf_op jit(solution)/shard_map/all_gather | solution.py:97
  73.4 2.9 select_reduce_fusion
  76.3 1.9 copy-done.2
  78.2 1.1 fusion.5
  79.3 49.4 %all-gather.5.cloned.1.call-done = bf16[4096,256]{1,0:T(8,128)(2,1)} async-done(((bf16[128,256]{1,0:T(8,128)(2,1)}), bf16[4096,256]{1,0:T(8,128)(2,1)}) %all-gather.5.cloned.1.call-update) | async-done | bytes 2097168 | tf_op jit(solution)/shard_map/all_gather | solution.py:98
  128.7 4.1 copy.95
  132.8 3.9 fusion.31
  136.7 1.1 convolution_convert_fusion
  137.9 4.3 scatter_custom_fusion
  142.3 74.3 %all-reduce.4.cloned.1.call-done = bf16[128,2048]{1,0:T(8,128)(2,1)} async-done(((bf16[128,2048]{1,0:T(8,128)(2,1)}), bf16[128,2048]{1,0:T(8,128)(2,1)}) %all-reduce.4.cloned.1.call-update) | async-done | bytes 524304 | tf_op jit(solution)/shard_map/psum | solution.py:144
  216.6 1.3 multiply_reduce_fusion
  217.9 1.3 multiply_convert_fusion
  219.2 0.8 copy-done.6
  220.0 7.1 %gather_fusion = bf16[1536,2048]{1,0:T(8,128)(2,1)} fusion(bf16[129,2048]{1,0:T(8,128)(2,1)S(1)} %concatenate.13, s32[2048]{0:T(1024)S(1)} %pad_clamp_fusion), kind=kCustom, calls=%fused_computation | custom fusion | bytes 12589056 | tf_op jit(solution)/shard_map/gather | solution.py:172
  227.1 149.0 %all_to_all.10 = bf16[32,2,24,2048]{3,2,1,0:T(8,128)(2,1)S(1)} all-to-all(bf16[32,2,24,2048]{3,2,1,0:T(8,128)(2,1)} %bitcast.85), channel_id=1, replica_groups=mesh['seq'=32,'tensor'=8] {'seq'}, dimensions={0} | all-to-all | bytes 12582912 | tf_op jit(solution)/shard_map/all_to_all | solution.py:173
  376.1 2.7 copy-done.5
  378.8 1.9 fusion.13
  380.7 8.9 %convert_bitcast_fusion = bf16[32,2,24,2048]{3,2,0,1:T(8,128)(2,1)} fusion(bf16[2,128,2048]{2,1,0:T(8,128)(2,1)S(1)} %copy-done, bf16[32,2,24,2048]{3,2,1,0:T(8,128)(2,1)} %copy-done.5, bf16[2,2048,128]{2,1,0:T(8,128)(2,1)S(1)} %copy-done.14, f32[32,2,24,128]{3,2,0,1:T(8,128)S(1)} %fusion.13), kind=kOutput, calls=%fused_computation.5 | convolution fusion | flops 1614938112 | bytes 15466496 | tf_op jit(solution)/shard_map/sjnf,jfd->sjnd/dot_general | solution.py:180
  389.6 6.6 %copy.84 = bf16[32,2,24,2048]{3,2,1,0:T(8,128)(2,1)} copy(bf16[32,2,24,2048]{3,2,0,1:T(8,128)(2,1)} %convert_bitcast_fusion) | data formatting | bytes 12582912 | tf_op jit(solution)/shard_map/convert_element_type | solution.py:182
  396.2 6.6 %all-to-all-start.1 = ((bf16[32,2,24,2048]{3,2,1,0:T(8,128)(2,1)}), bf16[32,2,24,2048]{3,2,1,0:T(8,128)(2,1)}, u32[]{:S(2)}, u32[]{:S(2)}) async-start(bf16[32,2,24,2048]{3,2,1,0:T(8,128)(2,1)} %copy.84), calls=%async_computation.1 | async-start | bytes 12582912 | tf_op jit(solution)/shard_map/all_to_all | solution.py:179
  402.8 0.3 all-reduce.6.cloned.1.call-start
  403.1 3.3 copy.86
  406.4 2.4 reshape.277
  408.8 4.1 copy.87
  412.8 0.3 fusion.81
  413.3 0.1 copy.85
  413.4 130.8 %all-to-all-done.1 = bf16[32,2,24,2048]{3,2,1,0:T(8,128)(2,1)} async-done(((bf16[32,2,24,2048]{3,2,1,0:T(8,128)(2,1)}), bf16[32,2,24,2048]{3,2,1,0:T(8,128)(2,1)}, u32[]{:S(2)}, u32[]{:S(2)}) %all-to-all-start.1) | async-done | bytes 6291488 | tf_op jit(solution)/shard_map/all_to_all | solution.py:179
  544.2 12.4 %gather_fusion.1 = bf16[1024,2048]{1,0:T(8,128)(2,1)} fusion(bf16[1536,2048]{1,0:T(8,128)(2,1)} %bitcast.22, s32[1024]{0:T(1024)S(1)} %broadcast_clamp_fusion), kind=kCustom, calls=%fused_computation.1 | custom fusion | bytes 8392704 | tf_op jit(solution)/shard_map/gather | solution.py:189
  556.6 7.5 %fusion = bf16[128,2048]{1,0:T(8,128)(2,1)} fusion(bf16[1024,2048]{1,0:T(8,128)(2,1)} %gather_fusion.1, f32[128,8]{1,0:T(8,128)S(1)} %copy.85), kind=kLoop, calls=%fused_computation.4 | loop fusion | flops 6029312 | bytes 4722688 | tf_op jit(solution)/shard_map/reduce_sum | solution.py:190
  564.1 2.2 convolution_convert_fusion.2
  566.3 0.7 copy.89
  567.0 2.4 reshape.278
  569.4 3.4 copy.88
  572.7 0.6 convolution_convert_fusion.1
  573.4 0.7 copy.90
  574.0 68.2 %all-reduce.6.cloned.1.call-done = bf16[128,2048]{1,0:T(8,128)(2,1)} async-done(((bf16[128,2048]{1,0:T(8,128)(2,1)}), bf16[128,2048]{1,0:T(8,128)(2,1)}) %all-reduce.6.cloned.1.call-update) | async-done | bytes 524304 | tf_op jit(solution)/shard_map/psum | solution.py:193
  642.2 2.4 add_convert_fusion
  (60 shorter events, 0.6 us)
Async XLA Ops:
  7.2 373.5 %copy-start = (bf16[2,128,2048]{2,1,0:T(8,128)(2,1)S(1)}, bf16[2,128,2048]{2,1,0:T(8,128)(2,1)}, u32[]{:S(2)}) copy-start(bf16[2,128,2048]{2,1,0:T(8,128)(2,1)} %param.27) | copy-start | bytes 3145732
  7.2 8.5 %copy-start.4 = (bf16[128,2048]{1,0:T(8,128)(2,1)S(1)}, bf16[128,2048]{1,0:T(8,128)(2,1)}, u32[]{:S(2)}) copy-start(bf16[128,2048]{1,0:T(8,128)(2,1)} %param.14) | copy-start | bytes 1572868
  7.2 8.5 %copy-start.15 = (f32[2048]{0:T(1024)S(1)}, f32[2048]{0:T(1024)}, u32[]{:S(2)}) copy-start(f32[2048]{0:T(1024)} %param.17) | copy-start | bytes 24580
  7.2 66.1 %all-gather.3.cloned.1.call-start = ((), (), s32[]{:S(2)}) async-start(), calls=%async_computation.2 | async-start | bytes 2162688 | tf_op jit(solution)/shard_map/all_gather | solution.py:97
  10.3 7.7 %copy-start.10 = (s32[128,8]{0,1:T(8,128)S(1)}, s32[128,8]{0,1:T(8,128)}, u32[]{:S(2)}) copy-start(s32[128,8]{0,1:T(8,128)} %param.24) | copy-start | bytes 12292
  15.6 113.1 %all-gather.5.cloned.1.call-start = ((), (), s32[]{:S(2)}) async-start(), calls=%async_computation.3 | async-start | bytes 2162688 | tf_op jit(solution)/shard_map/all_gather | solution.py:98
  17.9 198.7 %all-reduce.4.cloned.1.call-start = ((), (), s32[]{:S(2)}) async-start(), calls=%async_computation.4 | async-start | bytes 1048576 | tf_op jit(solution)/shard_map/psum | solution.py:144
  76.3 1.9 copy-start.2
  132.8 4.0 copy-start.8
  132.8 85.1 %copy-start.11 = (f32[2048]{0:T(1024)S(1)}, f32[2048]{0:T(1024)}, u32[]{:S(2)}) copy-start(f32[2048]{0:T(1024)} %param.22) | copy-start | bytes 24580
  219.2 0.8 copy-start.6
  227.1 151.7 %copy-start.13 = (bf16[2,2048,128]{2,1,0:T(8,128)(2,1)S(1)}, bf16[2,2048,128]{2,1,0:T(8,128)(2,1)}, u32[]{:S(2)}) copy-start(bf16[2,2048,128]{2,1,0:T(8,128)(2,1)} %param.25) | copy-start | bytes 3145732
  376.1 2.7 copy-start.5
  378.8 1.9 copy-start.14
  396.2 148.0 %all-to-all-start.1 = ((bf16[32,2,24,2048]{3,2,1,0:T(8,128)(2,1)}), bf16[32,2,24,2048]{3,2,1,0:T(8,128)(2,1)}, u32[]{:S(2)}, u32[]{:S(2)}) async-start(bf16[32,2,24,2048]{3,2,1,0:T(8,128)(2,1)} %copy.84), calls=%async_computation.1 | async-start | bytes 12582912 | tf_op jit(solution)/shard_map/all_to_all | solution.py:179
  402.8 239.4 %all-reduce.6.cloned.1.call-start = ((), (), s32[]{:S(2)}) async-start(), calls=%async_computation.5 | async-start | bytes 1048576 | tf_op jit(solution)/shard_map/psum | solution.py:193
  406.3 6.5 copy-start.7
  406.4 6.5 copy-start.9
  556.6 7.5 %copy-start.12 = (s32[256]{0:T(256)S(1)}, s32[256]{0:T(256)}, u32[]{:S(2)}) copy-start(s32[256]{0:T(256)} %param.16) | copy-start | bytes 3076
  556.6 10.4 %copy-start.3 = (bf16[4096,256]{1,0:T(8,128)(2,1)S(1)}, bf16[4096,256]{1,0:T(8,128)(2,1)}, u32[]{:S(2)}) copy-start(bf16[4096,256]{1,0:T(8,128)(2,1)} %all-gather.5.cloned.1.call-done) | copy-start | bytes 6291460
  569.3 75.2 %copy-start.1 = (bf16[2,128,2048]{2,1,0:T(8,128)(2,1)S(1)}, bf16[2,128,2048]{2,1,0:T(8,128)(2,1)}, u32[]{:S(2)}) copy-start(bf16[2,128,2048]{2,1,0:T(8,128)(2,1)} %param.27) | copy-start | bytes 3145732
Sparse Core Ops, SparseCore 0:
  15.7 57.5 all-gather.2
  76.5 52.1 all-gather.4
  138.0 78.5 all-reduce.3
  564.2 77.9 all-reduce.5
where the time goes:
time: 652 us; the launch traced here: 651 us
  waiting for transfers between devices  358 us (55%)
  blocking collectives  149 us (23%)
  local copies, waits for them, and re-layouts  58.9 us (9%)
  other arithmetic  36 us (6%)
  matrix products  27.7 us (4%)
  between operations  14.2 us (2%)
  starting transfers between devices  6.95 us (1%)
    all_to_all x1, blocking collectives, local(): lax.all_to_all(outgoing, 'seq', split_axis=0, concat_axis=0, tiled=True)  149 us
    all_to_all x1, waiting for transfers between devices, local(): lax.all_to_all(jnp.einsum('sjnf,jfd->sjnd', activation, down_weight, pref...  131 us
    psum x1, waiting for transfers between devices, local(): lax.psum(head_part.astype(jnp.bfloat16), 'tensor').astype(jnp.float32)  74.3 us
    psum x1, waiting for transfers between devices, local(): lax.psum(mixture_part.astype(jnp.bfloat16), 'tensor').astype(jnp.float32)  68.2 us
    all_gather x1, waiting for transfers between devices, local(): value_piece = lax.all_gather(value_rows, 'seq', axis=0, tiled=True)  49.4 us
    all_gather x1, waiting for transfers between devices, local(): key_piece = lax.all_gather(key_rows, 'seq', axis=0, tiled=True)  35.6 us
    another operation x5, other arithmetic  19.2 us
  transfers between devices with their start and end apart: 5, of which 5 were waited for; matrix products, arithmetic and copies ran while one was open for 8% of the time, Pallas kernels for 0%

commit v1 on v0

--- a/solution.py
+++ b/solution.py
@@ -94,8 +94,13 @@
         jnp.zeros((head_count, row_count), jnp.float32),
         jnp.zeros((head_count, row_count, HEAD_DIM), jnp.float32),
     )
-    key_piece = lax.all_gather(key_rows, "seq", axis=0, tiled=True)
-    value_piece = lax.all_gather(value_rows, "seq", axis=0, tiled=True)
+
+    def treat_samples(buf, array_in, a_name="seq"):
+        r_now = jnp.concatenate([buf, array_in], axis=1)
+        raw_out = lax.all_gather(r_now, axis_name=a_name, axis=0, tiled=True)
+        return jnp.split(raw_out, [buf.shape[1]], axis=1)
+
+    key_piece, value_piece = treat_samples(key_rows, value_rows)
     piece_rows = key_piece.shape[0]
     key_pages = jnp.dot(
         owned,

time: 652 us -> 607 us (0.931)
  waiting for transfers between devices: 358 us -> 319 us
    all_gather x2 -> x1, waiting for transfers between devices: 85 us -> 42.8 us  [treat_samples(): raw_out = lax.all_gather(r_now, axis_name=a_name, axis=0, tiled=True)]
  transfers between devices with their start and end apart: 5 -> 4, of which waited for: 5 -> 4; matrix products, arithmetic and copies ran while one was open for 8% -> 7% of each run, Pallas kernels for 0% -> 0%
where the time goes in v1:
time: 607 us
  waiting for transfers between devices  319 us (53%)
  blocking collectives  149 us (25%)
  local copies, waits for them, and re-layouts  55 us (9%)
  other arithmetic  37.5 us (6%)
  matrix products  24.7 us (4%)
  between operations  14.2 us (2%)
  starting transfers between devices  7.05 us (1%)
    all_to_all x1, blocking collectives, local(): lax.all_to_all(outgoing, 'seq', split_axis=0, concat_axis=0, tiled=True)  149 us
    all_to_all x1, waiting for transfers between devices, local(): lax.all_to_all(jnp.einsum('sjnf,jfd->sjnd', activation, down_weight, pref...  133 us
    psum x1, waiting for transfers between devices, local(): lax.psum(head_part.astype(jnp.bfloat16), 'tensor').astype(jnp.float32)  73.7 us
    psum x1, waiting for transfers between devices, local(): lax.psum(mixture_part.astype(jnp.bfloat16), 'tensor').astype(jnp.float32)  69.8 us
    all_gather x1, waiting for transfers between devices, treat_samples(): raw_out = lax.all_gather(r_now, axis_name=a_name, axis=0, tiled=True)  42.8 us
    another operation x5, other arithmetic  19.2 us
    gather x1, local copies, waits for them, and re-layouts, local(): picked = flat_rows[slot_index].astype(jnp.float32)  12.4 us
  transfers between devices with their start and end apart: 4, of which 4 were waited for; matrix products, arithmetic and copies ran while one was open for 7% of the time, Pallas kernels for 0%

profile of v1, /device:TPU:2, one launch (start us, length us, event | category | flops | bytes accessed | tf_op | source)
XLA Modules:
  0.0 606.5 jit_solution(626271273921527139)
XLA Ops:
  7.3 1.0 reduce-window.19
  8.3 0.7 bitcast_subtract_fusion
  8.9 0.1 convert_reduce_fusion.1
  9.0 0.1 select_reduce_fusion.2
  9.1 1.2 fusion.36
  10.4 1.8 convolution_convert_fusion.3
  12.1 1.8 fusion.77
  13.9 0.1 reshape.271
  14.0 0.4 fusion.79
  14.4 0.1 reshape.270
  14.4 0.3 multiply_cosine_fusion
  14.8 0.3 fusion.82
  15.1 0.1 subtract_convert_fusion.1
  15.2 0.1 copy_bitcast_fusion
  15.3 0.7 pad_maximum_fusion
  16.0 0.1 copy.79
  16.1 0.1 eq.91
  16.2 0.1 eq.87
  16.3 0.1 copy.78
  16.4 0.1 mul.205
  16.5 18.0 %reduce-window.20 = s32[64,8,128]{2,1,0:T(8,128)S(1)} reduce-window(s32[64,8,128]{2,1,0:T(8,128)S(1)} %fusion.54, s32[]{:T(128)} %constant.30.clone.1), window={size=1x1x128 pad=0_0x0_0x127_0}, to_apply=%region_9.10 | reduce-window | flops 8323072 | bytes 524292 | tf_op jit(solution)/shard_map/reduce-window.1
  34.6 0.1 slice.32
  34.7 0.1 copy.81
  34.9 0.1 copy.82
  35.0 0.1 convert_reduce_fusion
  35.1 0.1 broadcast_add_fusion
  35.2 0.1 fusion.53
  35.3 1.3 fusion.13
  36.6 42.8 %all-gather.2.cloned.1.call-done = bf16[4096,512]{1,0:T(8,128)(2,1)} async-done(((bf16[128,512]{1,0:T(8,128)(2,1)}), bf16[4096,512]{1,0:T(8,128)(2,1)}) %all-gather.2.cloned.1.call-update) | async-done | bytes 4194320 | tf_op jit(solution)/shard_map/all_gather | solution.py:100
  79.4 4.9 fusion.81
  84.3 2.9 copy.94
  87.2 3.1 select_reduce_fusion
  90.4 1.1 fusion.5
  91.5 1.0 fusion.33
  92.5 0.2 copy-done.12
  92.7 1.1 convolution_convert_fusion
  93.9 4.3 scatter_custom_fusion
  98.2 73.7 %all-reduce.4.cloned.1.call-done = bf16[128,2048]{1,0:T(8,128)(2,1)} async-done(((bf16[128,2048]{1,0:T(8,128)(2,1)}), bf16[128,2048]{1,0:T(8,128)(2,1)}) %all-reduce.4.cloned.1.call-update) | async-done | bytes 524304 | tf_op jit(solution)/shard_map/psum | solution.py:149
  171.9 1.3 multiply_reduce_fusion
  173.2 1.3 multiply_convert_fusion
  174.5 0.8 copy-done.8
  175.3 7.1 %gather_fusion = bf16[1536,2048]{1,0:T(8,128)(2,1)} fusion(bf16[129,2048]{1,0:T(8,128)(2,1)S(1)} %concatenate.17, s32[2048]{0:T(1024)S(1)} %pad_clamp_fusion), kind=kCustom, calls=%fused_computation | custom fusion | bytes 12589056 | tf_op jit(solution)/shard_map/gather | solution.py:177
  182.4 149.0 %all_to_all.10 = bf16[32,2,24,2048]{3,2,1,0:T(8,128)(2,1)S(1)} all-to-all(bf16[32,2,24,2048]{3,2,1,0:T(8,128)(2,1)} %bitcast.94), channel_id=1, replica_groups=mesh['seq'=32,'tensor'=8] {'seq'}, dimensions={0} | all-to-all | bytes 12582912 | tf_op jit(solution)/shard_map/all_to_all | solution.py:178
  331.4 2.7 copy-done.7
  334.0 1.9 fusion.15
  336.0 8.9 %convert_bitcast_fusion = bf16[32,2,24,2048]{3,2,0,1:T(8,128)(2,1)} fusion(bf16[2,128,2048]{2,1,0:T(8,128)(2,1)S(1)} %copy-done, bf16[32,2,24,2048]{3,2,1,0:T(8,128)(2,1)} %copy-done.7, bf16[2,2048,128]{2,1,0:T(8,128)(2,1)S(1)} %copy-done.19, f32[32,2,24,128]{3,2,0,1:T(8,128)S(1)} %fusion.15), kind=kOutput, calls=%fused_computation.5 | convolution fusion | flops 1614938112 | bytes 15466496 | tf_op jit(solution)/shard_map/sjnf,jfd->sjnd/dot_general | solution.py:185
  344.9 6.6 %copy.85 = bf16[32,2,24,2048]{3,2,1,0:T(8,128)(2,1)} copy(bf16[32,2,24,2048]{3,2,0,1:T(8,128)(2,1)} %convert_bitcast_fusion) | data formatting | bytes 12582912 | tf_op jit(solution)/shard_map/convert_element_type | solution.py:187
  351.5 6.7 %all-to-all-start.1 = ((bf16[32,2,24,2048]{3,2,1,0:T(8,128)(2,1)}), bf16[32,2,24,2048]{3,2,1,0:T(8,128)(2,1)}, u32[]{:S(2)}, u32[]{:S(2)}) async-start(bf16[32,2,24,2048]{3,2,1,0:T(8,128)(2,1)} %copy.85), calls=%async_computation.1 | async-start | bytes 12582912 | tf_op jit(solution)/shard_map/all_to_all | solution.py:184
  358.2 0.3 all-reduce.6.cloned.1.call-start
  358.5 2.4 reshape.278
  360.8 2.9 reshape.277
  363.8 2.5 copy.87
  366.3 0.3 fusion.84
  366.7 0.1 copy.86
  366.8 132.8 %all-to-all-done.1 = bf16[32,2,24,2048]{3,2,1,0:T(8,128)(2,1)} async-done(((bf16[32,2,24,2048]{3,2,1,0:T(8,128)(2,1)}), bf16[32,2,24,2048]{3,2,1,0:T(8,128)(2,1)}, u32[]{:S(2)}, u32[]{:S(2)}) %all-to-all-start.1) | async-done | bytes 6291488 | tf_op jit(solution)/shard_map/all_to_all | solution.py:184
  499.6 12.4 %gather_fusion.1 = bf16[1024,2048]{1,0:T(8,128)(2,1)} fusion(bf16[1536,2048]{1,0:T(8,128)(2,1)} %bitcast.20, s32[1024]{0:T(1024)S(1)} %broadcast_clamp_fusion), kind=kCustom, calls=%fused_computation.1 | custom fusion | bytes 8392704 | tf_op jit(solution)/shard_map/gather | solution.py:194
  512.0 7.5 %fusion = bf16[128,2048]{1,0:T(8,128)(2,1)} fusion(bf16[1024,2048]{1,0:T(8,128)(2,1)} %gather_fusion.1, f32[128,8]{1,0:T(8,128)S(1)} %copy.86), kind=kLoop, calls=%fused_computation.4 | loop fusion | flops 6029312 | bytes 4722688 | tf_op jit(solution)/shard_map/reduce_sum | solution.py:195
  519.5 2.2 convolution_convert_fusion.2
  521.7 0.7 copy.89
  522.4 2.5 copy.88
  524.9 2.2 convolution_convert_fusion.1
  527.1 0.7 copy.90
  527.8 69.8 %all-reduce.6.cloned.1.call-done = bf16[128,2048]{1,0:T(8,128)(2,1)} async-done(((bf16[128,2048]{1,0:T(8,128)(2,1)}), bf16[128,2048]{1,0:T(8,128)(2,1)}) %all-reduce.6.cloned.1.call-update) | async-done | bytes 524304 | tf_op jit(solution)/shard_map/psum | solution.py:198
  597.6 2.4 add_convert_fusion
  (67 shorter events, 0.5 us)
Async XLA Ops:
  7.2 328.8 %copy-start = (bf16[2,128,2048]{2,1,0:T(8,128)(2,1)S(1)}, bf16[2,128,2048]{2,1,0:T(8,128)(2,1)}, u32[]{:S(2)}) copy-start(bf16[2,128,2048]{2,1,0:T(8,128)(2,1)} %param.27) | copy-start | bytes 3145732
  7.2 6.8 %copy-start.5 = (bf16[128,2048]{1,0:T(8,128)(2,1)S(1)}, bf16[128,2048]{1,0:T(8,128)(2,1)}, u32[]{:S(2)}) copy-start(bf16[128,2048]{1,0:T(8,128)(2,1)} %param.14) | copy-start | bytes 1572868
  7.2 6.8 %copy-start.20 = (f32[2048]{0:T(1024)S(1)}, f32[2048]{0:T(1024)}, u32[]{:S(2)}) copy-start(f32[2048]{0:T(1024)} %param.17) | copy-start | bytes 24580
  7.2 6.8 %copy-start.17 = (bf16[2048,256]{1,0:T(8,128)(2,1)S(1)}, bf16[2048,256]{1,0:T(8,128)(2,1)}, u32[]{:S(2)}) copy-start(bf16[2048,256]{1,0:T(8,128)(2,1)} %param.18) | copy-start | bytes 3145732
  7.2 72.2 %all-gather.2.cloned.1.call-start = ((), (), s32[]{:S(2)}) async-start(), calls=%async_computation.2 | async-start | bytes 4325376 | tf_op jit(solution)/shard_map/all_gather | solution.py:100
  10.4 5.6 copy-start.14
  16.0 155.9 %all-reduce.4.cloned.1.call-start = ((), (), s32[]{:S(2)}) async-start(), calls=%async_computation.3 | async-start | bytes 1048576 | tf_op jit(solution)/shard_map/psum | solution.py:149
  84.3 6.0 copy-start.2
  87.2 3.1 copy-start.10
  87.2 4.2 copy-start.11
  91.5 1.2 copy-start.12
  91.5 80.4 %copy-start.6 = (bf16[128,2048]{1,0:T(8,128)(2,1)S(1)}, bf16[128,2048]{1,0:T(8,128)(2,1)}, u32[]{:S(2)}) copy-start(bf16[128,2048]{1,0:T(8,128)(2,1)} %param.14) | copy-start | bytes 1572868
  91.5 81.7 %copy-start.15 = (f32[2048]{0:T(1024)S(1)}, f32[2048]{0:T(1024)}, u32[]{:S(2)}) copy-start(f32[2048]{0:T(1024)} %param.22) | copy-start | bytes 24580
  174.4 0.8 copy-start.8
  182.4 151.7 %copy-start.18 = (bf16[2,2048,128]{2,1,0:T(8,128)(2,1)S(1)}, bf16[2,2048,128]{2,1,0:T(8,128)(2,1)}, u32[]{:S(2)}) copy-start(bf16[2,2048,128]{2,1,0:T(8,128)(2,1)} %param.25) | copy-start | bytes 3145732
  331.4 2.7 copy-start.7
  334.0 1.9 copy-start.19
  351.5 7.0 %copy-start.3 = (bf16[4096,256]{1,0:T(8,128)(2,1)S(1)}, bf16[4096,256]{1,0:T(8,128)(2,1)}, u32[]{:S(2)}) copy-start(bf16[4096,256]{1,0:T(8,128)(2,1)} %copy-done.2) | copy-start | bytes 6291460
  351.5 148.1 %all-to-all-start.1 = ((bf16[32,2,24,2048]{3,2,1,0:T(8,128)(2,1)}), bf16[32,2,24,2048]{3,2,1,0:T(8,128)(2,1)}, u32[]{:S(2)}, u32[]{:S(2)}) async-start(bf16[32,2,24,2048]{3,2,1,0:T(8,128)(2,1)} %copy.85), calls=%async_computation.1 | async-start | bytes 12582912 | tf_op jit(solution)/shard_map/all_to_all | solution.py:184
  358.2 239.4 %all-reduce.6.cloned.1.call-start = ((), (), s32[]{:S(2)}) async-start(), calls=%async_computation.4 | async-start | bytes 1048576 | tf_op jit(solution)/shard_map/psum | solution.py:198
  360.8 5.5 copy-start.9
  360.8 5.5 copy-start.13
  512.0 7.5 %copy-start.16 = (s32[256]{0:T(256)S(1)}, s32[256]{0:T(256)}, u32[]{:S(2)}) copy-start(s32[256]{0:T(256)} %param.16) | copy-start | bytes 3076
  512.0 10.4 %copy-start.4 = (bf16[256,4096]{1,0:T(8,128)(2,1)S(1)}, bf16[256,4096]{1,0:T(8,128)(2,1)}, u32[]{:S(2)}) copy-start(bf16[256,4096]{1,0:T(8,128)(2,1)} %reshape.278) | copy-start | bytes 6291460
  522.4 77.6 %copy-start.1 = (bf16[2,128,2048]{2,1,0:T(8,128)(2,1)S(1)}, bf16[2,128,2048]{2,1,0:T(8,128)(2,1)}, u32[]{:S(2)}) copy-start(bf16[2,128,2048]{2,1,0:T(8,128)(2,1)} %param.27) | copy-start | bytes 3145732
Sparse Core Ops, SparseCore 0:
  16.1 63.2 all-gather.1
  94.0 77.8 all-reduce.3
  519.6 77.9 all-reduce.5
